TPU v7x, 32 devices: a whole 2x2x4 slice. The times are simulated.
32 devices in a mesh: grp: 2 (over y), res: 4 (over z), br: 2 (over core), aux: 2 (over x).
Axes of the slice: x: 2, y: 2, z: 4, core: 2. Of those that a mesh axis runs over, the one named last changes fastest.
Arguments:
- homolog_features: bfloat16 [32, 128, 256], P(('grp', 'br', 'aux'), 'res'), parts along dimension 0, may hold values from -6 to 6
- couple_features: bfloat16 [256, 128, 128], P(('grp', 'res'), ('br', 'aux')), parts along dimension 0, may hold values from -6 to 6
- symbol_ids: int32 [32, 128], P(('grp', 'br', 'aux'), 'res'), parts along dimension 0, may hold values from 0 to 22
- entry_present: int32 [32, 128], P(('grp', 'br', 'aux'), 'res'), parts along dimension 0, may hold values 0 or 1
- amino_present: int32 [256], P('grp'), parts along dimension 0, may hold values 0 or 1
- symbol_lookup_matrix: bfloat16 [23, 256], replicated, may hold values from -3 to 3
- horizontal_entry_matrix: bfloat16 [256, 1024], replicated, may hold values from -0.375 to 0.375
- couple_logit_matrix: bfloat16 [128, 8], replicated, may hold values from -40 to 40, as said below
- horizontal_exit_matrix: bfloat16 [256, 256], replicated, may hold values from -0.375 to 0.375
- vertical_entry_matrix: bfloat16 [256, 1024], replicated, may hold values from -0.375 to 0.375
- vertical_exit_matrix: bfloat16 [256, 256], replicated, may hold values from -0.375 to 0.375
- feedforward_first_matrix: bfloat16 [256, 1024], replicated, may hold values from -0.375 to 0.375
- feedforward_second_matrix: bfloat16 [1024, 256], replicated, may hold values from -0.1875 to 0.1875
- trimul_entry_matrix: bfloat16 [128, 640], replicated, may hold values from -0.5 to 0.5
- trimul_exit_matrix: bfloat16 [128, 128], replicated, may hold values from -0.5 to 0.5
Outputs:
- alignment_output: bfloat16 [32, 128, 256], P(('grp', 'br', 'aux'), 'res'), parts along dimension 0
- pair_output: bfloat16 [256, 128, 128], P(('grp', 'res'), ('br', 'aux')), parts along dimension 0
There are 2 independent parts, one for each index of `grp`. A program takes and returns all parts, laid end to end along the dimension named above; an argument that names none is the same for every part. Nothing has to cross between parts.
Inputs may be any that keep to these rules, and one draw needn't show every extreme that they name: `couple_logit_matrix`: a projection of the 128 pair channels onto the 8 heads.
All inputs are finite; a program needn't handle non-finite values. No bound on the sum of `entry_present` on one device may be relied on, other than what follows from the above.
Results may differ from a plain program's by a relative error of at most 0.008.
Values may be sent and summed in bfloat16 or wider, within the bound.
A program may use at most 64 MiB of HBM per device.

v0:
```python
import functools

import jax
import jax.numpy as jnp
from jax import lax
from jax.experimental import pallas as pl
from jax.experimental.pallas import tpu as pltpu
from jax.sharding import PartitionSpec as P

epsilon = 1e-05
masked_fill_value = 1000000000.0
MESH = pl.DeviceIdType.MESH
f32 = jnp.float32
bf16 = jnp.bfloat16


def normalize(inputs, axis=-1):
    values = inputs.astype(f32)
    average = jnp.mean(values, axis=axis, keepdims=True)
    centred = values - average
    variance = jnp.mean(centred * centred, axis=axis, keepdims=True)
    return centred * lax.rsqrt(variance + epsilon)


def dot(a, b, contract):
    return lax.dot_general(a, b, (contract, ((), ())), preferred_element_type=f32)


class Peers:
    def __init__(self, sizes):
        self.R, self.BR, self.AX = sizes
        self.r = lax.axis_index("res")
        self.b = lax.axis_index("br")
        self.x = lax.axis_index("aux")

    def res(self, d):
        return lax.rem(self.r + d, self.R)

    def br(self, d):
        return lax.rem(self.b + d, self.BR)

    def aux(self, d):
        return lax.rem(self.x + d, self.AX)

    def res_back(self, d):
        return lax.rem(self.r + self.R - d, self.R)

    def aux_back(self, d):
        return lax.rem(self.x + self.AX - d, self.AX)

    def group(self):
        return [(bo, a) for bo in range(self.BR) for a in range(self.AX) if (bo, a) != (0, 0)]

    def greet(self):
        semaphore = pltpu.get_barrier_semaphore()
        for d in range(1, self.R):
            pl.semaphore_signal(semaphore, inc=1, device_id={"res": self.res(d)}, device_id_type=MESH)
        for bo, a in self.group():
            pl.semaphore_signal(
                semaphore, inc=1, device_id={"br": self.br(bo), "aux": self.aux(a)}, device_id_type=MESH
            )

    def met(self):
        pl.semaphore_wait(pltpu.get_barrier_semaphore(), self.R - 1 + self.BR * self.AX - 1)


def remote(src, dst, send, recv, device):
    copy = pltpu.make_async_remote_copy(
        src_ref=src, dst_ref=dst, send_sem=send, recv_sem=recv, device_id=device, device_id_type=MESH
    )
    copy.start()
    return copy


def iota(shape, axis):
    return lax.broadcasted_iota(jnp.int32, shape, axis)


def by_head(rows, heads):
    n, width = rows.shape
    mask = (iota((heads, width), 1) // (width // heads) == iota((heads, width), 0)).astype(f32)
    return (rows[:, None, :] * mask[None]).reshape(n * heads, width)


def from_head(rows, heads):
    n, width = rows.shape
    mask = (iota((heads, width), 1) // (width // heads) == iota((heads, width), 0)).astype(f32)
    return jnp.sum(rows.reshape(n // heads, heads, width) * mask[None], axis=1)


def attend(scores, values, heads):
    powers = jnp.exp(scores - jnp.max(scores, axis=-1, keepdims=True))
    total = jnp.sum(powers, axis=-1, keepdims=True)
    mixed = dot(powers.astype(bf16), values, ((1,), (0,)))
    return from_head(mixed / total, heads)


def joined(pieces, lanes):
    per_tile = 128 // lanes
    tiles = []
    for first in range(0, len(pieces), per_tile):
        tile = pieces[first]
        group = iota(tile.shape, 1) // lanes
        for k in range(1, min(per_tile, len(pieces) - first)):
            tile = jnp.where(group == k, pieces[first + k], tile)
        tiles.append(tile)
    return tiles[0] if len(tiles) == 1 else jnp.concatenate(tiles, axis=1)


def block_kernel(
    sizes, dims,
    homolog, couple, symbols, entries, amino, table, logit, tri_in, tri_exit,
    row_in_far, row_exit_far, col_in_far, col_exit_far, feed_first_far, feed_second_far,
    alignment, pair,
    rows_own, bias_own, left_own, right_own, keys_own, product_own,
    rows_all, row_present, bias_all, col_present, left_all, right_all, keys_all, product_all,
    row_in, row_exit, col_in, col_exit, feed_first, feed_second, present,
    embedded_s, pair_norm_s, gate_s, bias_s, key_value_s, left_s, right_s, product_s, update_s, context_s,
    res_send, res_recv, grp_send, grp_recv, aux_send, aux_recv, br_send, br_recv,
    across_send, across_recv, over_send, over_recv, weight_sem,
):
    p = Peers(sizes)
    R, BR, AX = sizes
    B = BR * AX
    S, A, F, H, I, J, C, per, T, N = dims
    scale = (F // H) ** (-0.5)
    Q = 128 // J
    M = J // Q
    p.greet()
    weights = []
    for n, (far, near) in enumerate(
        (
            (row_in_far, row_in),
            (row_exit_far, row_exit),
            (col_in_far, col_in),
            (col_exit_far, col_exit),
            (feed_first_far, feed_first),
            (feed_second_far, feed_second),
        )
    ):
        weights.append(pltpu.make_async_copy(far, near, weight_sem.at[n]))
        weights[n].start()
    sent = []
    arriving = {"rows": [], "bias": [], "right": [], "left": [], "keys": [], "product": []}

    pair_norm = normalize(couple[...]).astype(bf16)
    pair_norm_s[...] = pair_norm
    alive = jnp.broadcast_to(amino[...].astype(f32), (8, amino.shape[1])).astype(bf16)
    residue = iota((amino.shape[1], I * J), 0)
    flat = iota((amino.shape[1], I * J), 1)
    row_pick = (residue == p.r * I + flat // J).astype(f32).astype(bf16)
    col_pick = (residue == (p.b * AX + p.x) * J + flat % J).astype(f32).astype(bf16)
    pair_valid = (dot(alive, row_pick, ((1,), (0,))) * dot(alive, col_pick, ((1,), (0,))))[:1]
    turned_in = [jnp.transpose(tri_in[:, n * C : (n + 1) * C].astype(f32)).astype(bf16) for n in range(4)]
    for side, own in ((0, left_own), (1, right_own)):
        value = dot(turned_in[2 * side], pair_norm, ((1,), (1,)))
        sigma = jax.nn.sigmoid(dot(turned_in[2 * side + 1], pair_norm, ((1,), (1,))))
        value = sigma * value * pair_valid
        for n in range(R):
            for t in range(T):
                own[n, t] = value[n * per : (n + 1) * per, t * 128 : (t + 1) * 128].astype(bf16)
    bias_own[...] = dot(jnp.transpose(logit[...].astype(f32)).astype(bf16), pair_norm, ((1,), (1,)))
    here = entries[...].astype(f32)
    present[...] = jnp.zeros_like(present)
    present[0, :S, :] = jnp.concatenate([here] * (128 // A), axis=1)
    for g in range(A // N):
        pieces = [here[s : s + 1, g * N : (g + 1) * N] for s in range(S)]
        present[1, g : g + 1, :] = jnp.concatenate(pieces * (128 // (S * N)), axis=1)
    tokens = table.shape[0]
    for s in range(S):
        chosen = (iota((tokens, A), 0) == symbols[s : s + 1, :]).astype(f32)
        context_s[s * A : (s + 1) * A, :] = dot(jnp.transpose(chosen).astype(bf16), table[...], ((1,), (0,)))
    embedded = homolog[...].astype(f32) + context_s[...]
    embedded_s[...] = embedded
    normed_first = normalize(embedded).astype(bf16)
    rows_own[...] = normed_first

    p.met()

    def relay(d, a):
        origin = (p.b, p.aux_back(a), p.res_back(d))
        src = left_own.at[p.r] if (d, a) == (0, 0) else left_all.at[origin]
        for bo in range(1, BR):
            copy = remote(
                src, left_all.at[origin], br_send.at[d, a, bo], br_recv.at[d, a, bo], {"br": p.br(bo)}
            )
            sent.append(copy)
            arriving["left"].append(copy)

    def spread(d):
        origin = (p.b, p.x, p.res_back(d))
        src = left_own.at[p.r] if d == 0 else left_all.at[origin]
        copies = {}
        for a in range(1, AX):
            copies[a] = remote(
                src, left_all.at[origin], aux_send.at[d, a], aux_recv.at[d, a], {"aux": p.aux(a)}
            )
            sent.append(copies[a])
        relay(d, 0)
        return copies

    def to_res(index, kind, pairs):
        for d in range(1, R):
            for n, (src, dst) in enumerate(pairs(p.res(d))):
                copy = remote(
                    src, dst, res_send.at[index + n, d], res_recv.at[index + n, d], {"res": p.res(d)}
                )
                sent.append(copy)
                arriving[kind].append(copy)

    lefts = {}
    for d in range(1, R):
        lefts[d] = remote(
            left_own.at[p.res(d)], left_all.at[p.b, p.x, p.r], res_send.at[0, d], res_recv.at[0, d],
            {"res": p.res(d)},
        )
        sent.append(lefts[d])
    spreads = {0: spread(0)}
    to_res(1, "rows", lambda to: ((rows_own, rows_all.at[p.r]), (present.at[0], row_present.at[p.r])))
    for n, (bo, a) in enumerate(p.group()):
        to = {"br": p.br(bo), "aux": p.aux(a)}
        for m, (src, dst) in enumerate(((bias_own, bias_all), (present.at[1], col_present))):
            copy = remote(src, dst.at[p.b, p.x], grp_send.at[m, n], grp_recv.at[m, n], to)
            sent.append(copy)
            arriving["bias"].append(copy)
    to_res(3, "right", lambda to: ((right_own.at[to], right_all.at[p.r]),))
    rows_all[p.r] = rows_own[...]
    row_present[p.r] = present[0]
    bias_all[p.b, p.x] = bias_own[...]
    col_present[p.b, p.x] = present[1]
    left_all[p.b, p.x, p.r] = left_own[p.r]
    right_all[p.r] = right_own[p.r]

    weights[0].wait()
    query = dot(normed_first, row_in[:, :F], ((1,), (0,))).astype(bf16).astype(f32)
    row_gate = jax.nn.sigmoid(dot(normed_first, row_in[:, 3 * F :], ((1,), (0,))))
    gate_s[...] = jax.nn.sigmoid(dot(pair_norm, tri_in[:, 4 * C :], ((1,), (0,))))

    for d in range(1, R):
        lefts[d].wait_recv()
        spreads[d] = spread(d)
    for copy in arriving["bias"]:
        copy.wait_recv()
    for t in range(T):
        for q in range(Q):
            pieces = []
            for b in range(B):
                tile = bias_all[b // AX, b % AX, :, t * 128 : (t + 1) * 128]
                turn = (b - q) % Q * J
                pieces.append(pltpu.roll(tile, turn, 1) if turn else tile)
            row = (t * Q + q) * H
            bias_s[row : row + H, :] = joined(pieces, J)
    for d in range(R):
        for a in range(1, AX):
            spreads[d][a].wait_recv()
            relay(d, a)

    for copy in arriving["rows"]:
        copy.wait_recv()
    key_value_s[...] = (
        dot(rows_all[...].reshape(R * S * A, F), row_in[:, F : 3 * F], ((1,), (0,)))
        .astype(bf16)
        .reshape(R, S * A, 2 * F)
    )
    presence = joined([row_present[n] for n in range(R)], A)
    for s in range(S):
        mine = slice(s * A, (s + 1) * A)
        keys = key_value_s[:, mine, :F].reshape(R * A, F)
        values = key_value_s[:, mine, F:].reshape(R * A, F)
        scores = dot(by_head(query[mine], H).astype(bf16), keys, ((1,), (1,))) * scale
        scores = scores + bias_s[...] + masked_fill_value * (presence[s : s + 1] - 1.0)
        context_s[mine, :] = attend(scores, values, H)
    weights[1].wait()
    weights[2].wait()
    row_mix = (row_gate * context_s[...]).astype(bf16)
    after_row = embedded_s[...] + dot(row_mix, row_exit[...], ((1,), (0,)))
    normed_second = normalize(after_row).astype(bf16)
    keys_own[...] = dot(normed_second, col_in[:, F : 3 * F], ((1,), (0,))).astype(bf16).reshape(S, A, 2 * F)
    query = dot(normed_second, col_in[:, :F], ((1,), (0,))).astype(bf16).astype(f32)
    col_gate = jax.nn.sigmoid(dot(normed_second, col_in[:, 3 * F :], ((1,), (0,))))

    def pass_on(a):
        origin = (p.b, p.aux_back(a))
        src = keys_own if a == 0 else keys_all.at[origin]
        for bo in range(1, BR):
            copy = remote(src, keys_all.at[origin], over_send.at[a, bo], over_recv.at[a, bo], {"br": p.br(bo)})
            sent.append(copy)
            arriving["keys"].append(copy)

    across = {}
    for a in range(1, AX):
        across[a] = remote(
            keys_own, keys_all.at[p.b, p.x], across_send.at[a], across_recv.at[a], {"aux": p.aux(a)}
        )
        sent.append(across[a])
    pass_on(0)
    keys_all[p.b, p.x] = keys_own[...]

    for copy in arriving["right"]:
        copy.wait_recv()
    right_s[...] = right_all[...].astype(f32).reshape(R * T * per, 128)
    for copy in arriving["left"]:
        copy.wait_recv()
    for b in range(B):
        left_s[b] = left_all[b // AX, b % AX].astype(f32).reshape(R * T * per, 128)
    wide = iota((J, 128), 1) // J
    lane = iota((M, 128), 1)

    def channel(c, carry):
        pick = pl.ds(c, R * T, stride=per)
        right = jnp.transpose(right_s[pick, :]).astype(bf16)
        lefts = jnp.concatenate([left_s[b, pick, :].astype(bf16) for b in range(B)], axis=1)
        grid = dot(right, lefts, ((1,), (0,)))
        for b in range(B):
            tile = grid[:, b * 128 : (b + 1) * 128]
            folded = tile[:J]
            for q in range(1, Q):
                folded = jnp.where(wide == q, tile[q * J : (q + 1) * J], folded)
            pieces = [folded[g * M : (g + 1) * M] for g in range(Q)]
            turn = J
            while turn < 128:
                low = (lane & turn) == 0
                pieces = [
                    jnp.where(low, pieces[k], pieces[k + 1])
                    + pltpu.roll(jnp.where(low, pieces[k + 1], pieces[k]), turn, 1)
                    for k in range(0, len(pieces), 2)
                ]
                turn *= 2
            product_s[b, pl.ds(pl.multiple_of(c * M, M), M), :] = pieces[0]
        return carry

    lax.fori_loop(0, per, channel, 0, unroll=4)
    product_own[...] = product_s[...].astype(bf16)
    for a in range(1, AX):
        across[a].wait_recv()
        pass_on(a)
    to_res(4, "product", lambda to: ((product_own.at[to], product_all.at[p.r]),))
    product_all[p.r] = product_own[p.r]

    for copy in arriving["keys"]:
        copy.wait_recv()
    presence = joined([col_present[b // AX, b % AX] for b in range(B)], S * N)
    for g in range(A // N):
        keys = keys_all[:, :, :, g * N : (g + 1) * N, :F].reshape(B * S * N, F)
        values = keys_all[:, :, :, g * N : (g + 1) * N, F:].reshape(B * S * N, F)
        rows = jnp.concatenate([query[s * A + g * N : s * A + (g + 1) * N] for s in range(S)], axis=0)
        scores = dot(by_head(rows, H).astype(bf16), keys, ((1,), (1,))) * scale
        scores = scores + masked_fill_value * (presence[g : g + 1] - 1.0)
        scores = jnp.where(iota(scores.shape, 0) // H % N == iota(scores.shape, 1) % N, scores, -1e30)
        context = attend(scores, values, H)
        for s in range(S):
            context_s[s * A + g * N : s * A + (g + 1) * N, :] = context[s * N : (s + 1) * N]
    for n in (3, 4, 5):
        weights[n].wait()
    col_mix = (col_gate * context_s[...]).astype(bf16)
    after_col = after_row + dot(col_mix, col_exit[...], ((1,), (0,)))
    normed_third = normalize(after_col).astype(bf16)
    hidden = jnp.maximum(dot(normed_third, feed_first[...], ((1,), (0,))), 0.0).astype(bf16)
    alignment[...] = (after_col + dot(hidden, feed_second[...], ((1,), (0,)))).astype(bf16)

    for copy in arriving["product"]:
        copy.wait_recv()
    normed = normalize(product_all[...].astype(f32).reshape(C, M, 128), axis=0)
    final_s = left_s.at[0]
    final_s[: C * M, :] = normed.reshape(C * M, 128)
    for m in range(M):
        turned = jnp.transpose(final_s[pl.ds(m, C, stride=M), :]).astype(bf16)
        update = dot(turned, tri_exit[...], ((1,), (0,)))
        for g in range(Q):
            update_s[pl.ds(g * M + m, I, stride=J), :] = update[g * I : (g + 1) * I]
    pair[...] = (couple[...].astype(f32) + gate_s[...] * update_s[...]).astype(bf16)
    for copy in sent:
        copy.wait_send()


def on_device(
    sizes,
    homolog_features,
    couple_features,
    symbol_ids,
    entry_present,
    amino_present,
    symbol_lookup_matrix,
    horizontal_entry_matrix,
    couple_logit_matrix,
    horizontal_exit_matrix,
    vertical_entry_matrix,
    vertical_exit_matrix,
    feedforward_first_matrix,
    feedforward_second_matrix,
    trimul_entry_matrix,
    trimul_exit_matrix,
):
    R, BR, AX = sizes
    B = BR * AX
    S, A, F = homolog_features.shape
    H = couple_logit_matrix.shape[1]
    I, J, C = couple_features.shape
    per = C // R
    T = I * J // 128
    N = 16
    assert I == J and R == B and 128 % J == 0 and 128 % A == 0 and 128 % (S * N) == 0 and A % N == 0
    M = J // (128 // J)
    near = (
        homolog_features.reshape(S * A, F),
        couple_features.reshape(I * J, C),
        symbol_ids,
        entry_present,
        amino_present.reshape(1, -1),
        symbol_lookup_matrix,
        couple_logit_matrix,
        trimul_entry_matrix,
        trimul_exit_matrix,
    )
    far = (
        horizontal_entry_matrix,
        horizontal_exit_matrix,
        vertical_entry_matrix,
        vertical_exit_matrix,
        feedforward_first_matrix,
        feedforward_second_matrix,
    )
    vmem = pl.BlockSpec(memory_space=pltpu.VMEM)
    buffers = [
        ((S * A, F), bf16), ((H, I * J), f32), ((R, T, per, 128), bf16), ((R, T, per, 128), bf16),
        ((S, A, 2 * F), bf16), ((R, per * M, 128), bf16),
        ((R, S * A, F), bf16), ((R, 8, 128), f32), ((BR, AX, H, I * J), f32), ((BR, AX, 8, 128), f32),
        ((BR, AX, R, T, per, 128), bf16), ((R, T, per, 128), bf16), ((BR, AX, S, A, 2 * F), bf16),
        ((R, per * M, 128), bf16),
        *[(weight.shape, bf16) for weight in far], ((2, 8, 128), f32),
        ((S * A, F), f32), ((I * J, C), bf16), ((I * J, C), f32), ((I * H, B * J), f32),
        ((R, S * A, 2 * F), bf16), ((B, R * T * per, 128), f32), ((R * T * per, 128), f32),
        ((R, per * M, 128), f32), ((I * J, C), f32), ((S * A, F), f32),
    ]
    semaphores = [
        (5, R), (5, R), (2, B), (2, B), (R, AX), (R, AX), (R, AX, BR), (R, AX, BR),
        (AX,), (AX,), (AX, BR), (AX, BR), (len(far),),
    ]
    alignment, pair = pl.pallas_call(
        functools.partial(block_kernel, sizes, (S, A, F, H, I, J, C, per, T, N)),
        name="block",
        out_shape=[jax.ShapeDtypeStruct((S * A, F), bf16), jax.ShapeDtypeStruct((I * J, C), bf16)],
        in_specs=[vmem] * len(near) + [pl.BlockSpec(memory_space=pl.ANY)] * len(far),
        out_specs=[vmem] * 2,
        scratch_shapes=[pltpu.VMEM(*b) for b in buffers] + [pltpu.SemaphoreType.DMA(s) for s in semaphores],
        compiler_params=pltpu.CompilerParams(
            collective_id=1, has_side_effects=True, vmem_limit_bytes=60 * 1024 * 1024
        ),
    )(*near, *far)
    return (alignment.reshape(S, A, F), pair.reshape(I, J, C))


def solution(mesh):
    sizes = (mesh.shape["res"], mesh.shape["br"], mesh.shape["aux"])
    return jax.shard_map(
        functools.partial(on_device, sizes),
        mesh=mesh,
        in_specs=(
            P(("grp", "br", "aux"), "res", None),
            P(("grp", "res"), ("br", "aux"), None),
            P(("grp", "br", "aux"), "res"),
            P(("grp", "br", "aux"), "res"),
            P("grp"),
        )
        + (P(),) * 10,
        out_specs=(P(("grp", "br", "aux"), "res", None), P(("grp", "res"), ("br", "aux"), None)),
        check_vma=False,
    )
```

profile of v0, /device:TPU:0, one launch (start us, length us, event | category | flops | bytes accessed | tf_op | source)
XLA Modules:
  0.0 42.2 jit_solution(14047017211953088407)
XLA Ops:
  0.6 0.0 copy-start
  0.6 0.7 %copy-done = bf16[128,8]{0,1:T(8,128)(2,1)S(1)} copy-done((bf16[128,8]{0,1:T(8,128)(2,1)S(1)}, bf16[128,8]{0,1:T(8,128)(2,1)}, u32[]{:S(2)}) %copy-start) | copy-done | bytes 2072
  1.3 0.7 %copy.17.logit = bf16[128,8]{1,0:T(8,128)(2,1)} copy(bf16[128,8]{0,1:T(8,128)(2,1)S(1)} %copy-done) | data formatting | bytes 4096 | tf_op args[7]
  2.0 37.0 %block.1 = (bf16[128,256]{1,0:T(8,128)(2,1)}, bf16[1024,128]{1,0:T(8,128)(2,1)}) custom-call(bf16[128,256]{1,0:T(8,128)(2,1)} %bitcast.7, bf16[1024,128]{1,0:T(8,128)(2,1)} %bitcast.5, s32[4,32]{1,0:T(4,128)} %symbols.1, s32[4,32]{1,0:T(4,128)} %entries.1, s32[1,128]{1,0:T(1,128)} %bitcast.9, bf16[23,256]{1,0:T(8,128)(2,1)} %table.1, ...), custom_call_target="tpu_custom_call" | custom-call | tf_op jit(solution)/shard_map/block/pallas_call | solution.py:439
  39.1 1.5 %copy.20 = bf16[4,32,256]{2,1,0:T(8,128)(2,1)} copy(bf16[4,32,256]{2,1,0:T(8,128)(2,1)} %bitcast.8) | data formatting | bytes 131072
  40.5 1.7 %copy.21 = bf16[32,32,128]{2,1,0:T(8,128)(2,1)} copy(bf16[32,32,128]{2,1,0:T(8,128)(2,1)} %bitcast.6) | data formatting | bytes 524288
Async XLA Ops:
  0.6 0.7 %copy-start = (bf16[128,8]{0,1:T(8,128)(2,1)S(1)}, bf16[128,8]{0,1:T(8,128)(2,1)}, u32[]{:S(2)}) copy-start(bf16[128,8]{0,1:T(8,128)(2,1)} %param.22) | copy-start | bytes 6148
where the time goes:
time: 42.4 us; the launch traced here: 42.2 us
  Pallas kernels  37 us (87%)
  local copies, waits for them, and re-layouts  4.54 us (11%)
  between operations  0.65 us (2%)
    pallas_call x1, Pallas kernels, on_device(): pl.pallas_call(functools.partial(block_kernel, sizes, (S, A, F, H, I, J,...  37 us
    unnamed x5, local copies, waits for them, and re-layouts  4.54 us

commit v1 on v0

--- a/solution.py
+++ b/solution.py
@@ -1,4 +1,5 @@
 import functools
+import types
 
 import jax
 import jax.numpy as jnp
@@ -373,6 +374,332 @@
         copy.wait_send()
 
 
+def lane_exchange(pieces, width):
+    count = len(pieces)
+    step = 1
+    while step < count:
+        lower = (iota(pieces[0].shape, pieces[0].ndim - 1) // width // step) % 2 == 0
+        axis = pieces[0].ndim - 1
+        turned = list(pieces)
+        for n in range(count):
+            if n // step % 2 == 0:
+                first, second = pieces[n], pieces[n + step]
+                turned[n] = jnp.where(lower, first, pltpu.roll(second, step * width, axis))
+                turned[n + step] = jnp.where(lower, pltpu.roll(first, 128 - step * width, axis), second)
+        pieces = turned
+        step *= 2
+    return pieces
+
+
+def exchange_kernel(sizes, dims, names, *refs):
+    v = types.SimpleNamespace(**dict(zip(names, refs, strict=True)))
+    p = Peers(sizes)
+    R, BR, AX = sizes
+    B = BR * AX
+    D = R * B
+    S, A, F, H, I, J, C, P4, T, N, rounds = dims
+    scale = (F // H) ** (-0.5)
+    Q = 128 // J
+    M = J // Q
+    peers = [(d, bo, a) for d in far_first(R) for bo in range(BR) for a in range(AX) if (d, bo, a) != (0, 0, 0)]
+    loads = {}
+    for n, name in enumerate(INPUTS):
+        loads[name] = pltpu.make_async_copy(getattr(v, name + "_far"), getattr(v, name), v.load_sem.at[n])
+        loads[name].start()
+    barrier = pltpu.get_barrier_semaphore()
+    for d, bo, a in peers:
+        pl.semaphore_signal(
+            barrier, inc=1, device_id={"res": p.res(d), "br": p.br(bo), "aux": p.aux(a)}, device_id_type=MESH
+        )
+    sent = []
+    arriving = {"rows": [], "bias": [], "keys": []}
+
+    def chosen_weights(h, gate):
+        row = iota((2 * P4 * D, 1), 0)
+        want = (2 * (row // P4 % 2) + gate) * C + h * P4 * D + row // (2 * P4) * P4 + row % P4
+        pick = (iota((2 * P4 * D, 4 * C), 1) == want).astype(f32).astype(bf16)
+        return dot(pick, v.tri_in[:, : 4 * C], ((1,), (1,))).astype(bf16)
+
+    def operands(h, pair_norm):
+        value = dot(chosen_weights(h, 0), pair_norm, ((1,), (1,)))
+        value = value * jax.nn.sigmoid(dot(chosen_weights(h, 1), pair_norm, ((1,), (1,))))
+        for n in range(D):
+            for t in range(0, T, 2):
+                two = [value[n * 2 * P4 : (n + 1) * 2 * P4, u * 128 : (u + 1) * 128] for u in (t, t + 1)]
+                v.side_own[h, n // B, n // AX % BR, n % AX, t * 8 : t * 8 + 16, :] = jnp.concatenate(two, axis=0).astype(bf16)
+
+    def share(own, everyone, send, recv, h):
+        copies = []
+        for n, (d, bo, a) in enumerate(peers):
+            to = (p.res(d), p.br(bo), p.aux(a))
+            copy = remote(
+                own.at[(h, *to)], everyone.at[h, p.b, p.x, p.r] if everyone is v.side_all else everyone.at[h, p.r, p.b, p.x],
+                send.at[h, n], recv.at[h, n], {"res": to[0], "br": to[1], "aux": to[2]},
+            )
+            copies.append(copy)
+            sent.append(copy)
+        return copies
+
+    loads["couple"].wait()
+    loads["tri_in"].wait()
+    pair_norm = normalize(v.couple[...]).astype(bf16)
+    v.pair_norm_s[...] = pair_norm
+    operands(0, pair_norm)
+    pl.semaphore_wait(barrier, D - 1)
+    sides = {0: share(v.side_own, v.side_all, v.side_send, v.side_recv, 0)}
+
+    for name in ("homolog", "symbols", "entries", "table"):
+        loads[name].wait()
+    here = v.entries[...].astype(f32)
+    v.present[...] = jnp.zeros_like(v.present)
+    v.present[0, :S, :] = jnp.concatenate([here] * (128 // A), axis=1)
+    for g in range(A // N):
+        pieces = [here[s : s + 1, g * N : (g + 1) * N] for s in range(S)]
+        v.present[1, g : g + 1, :] = jnp.concatenate(pieces * (128 // (S * N)), axis=1)
+    tokens = v.table.shape[0]
+    for s in range(S):
+        chosen = (iota((tokens, A), 0) == v.symbols[s : s + 1, :]).astype(f32)
+        v.context_s[s * A : (s + 1) * A, :] = dot(jnp.transpose(chosen).astype(bf16), v.table[...], ((1,), (0,)))
+    embedded = v.homolog[...].astype(f32) + v.context_s[...]
+    v.embedded_s[...] = embedded
+    normed_first = normalize(embedded).astype(bf16)
+    v.rows_own[...] = normed_first
+    for d in far_first(R):
+        if d:
+            for n, (src, dst) in enumerate(((v.rows_own, v.rows_all), (v.present.at[0], v.row_present))):
+                copy = remote(src, dst.at[p.r], v.row_send.at[n, d], v.row_recv.at[n, d], {"res": p.res(d)})
+                sent.append(copy)
+                arriving["rows"].append(copy)
+    loads["logit"].wait()
+    v.bias_own[...] = dot(v.logit[...], pair_norm, ((1,), (1,)))
+    for n, (bo, a) in enumerate(p.group()):
+        to = {"br": p.br(bo), "aux": p.aux(a)}
+        for m, (src, dst) in enumerate(((v.bias_own, v.bias_all), (v.present.at[1], v.col_present))):
+            copy = remote(src, dst.at[p.b, p.x], v.grp_send.at[m, n], v.grp_recv.at[m, n], to)
+            sent.append(copy)
+            arriving["bias"].append(copy)
+    for h in range(1, rounds):
+        operands(h, v.pair_norm_s[...])
+        sides[h] = share(v.side_own, v.side_all, v.side_send, v.side_recv, h)
+
+    v.rows_all[p.r] = v.rows_own[...]
+    v.row_present[p.r] = v.present[0]
+    v.bias_all[p.b, p.x] = v.bias_own[...]
+    v.col_present[p.b, p.x] = v.present[1]
+    for h in range(rounds):
+        v.side_all[h, p.b, p.x, p.r] = v.side_own[h, p.r, p.b, p.x]
+
+    loads["row_in"].wait()
+    query = dot(normed_first, v.row_in[:, :F], ((1,), (0,))).astype(bf16).astype(f32)
+    row_gate = jax.nn.sigmoid(dot(normed_first, v.row_in[:, 3 * F :], ((1,), (0,))))
+    v.gate_s[...] = jax.nn.sigmoid(dot(v.pair_norm_s[...], v.tri_in[:, 4 * C :], ((1,), (0,))))
+    loads["amino"].wait()
+    alive = v.amino[...].astype(f32)
+    line = iota((128, 128), 0)
+    lane = iota((128, 128), 1)
+    alive_rows = jnp.sum(jnp.where(lane == line, alive, 0.0), axis=1, keepdims=True)
+    depth = line % (R * T)
+    alive_depth = jnp.sum(jnp.where(lane == depth // T * I + depth % T * Q + line // (R * T), alive, 0.0), axis=1, keepdims=True)
+    v.depth_valid_s[...] = jnp.broadcast_to(alive_depth, (128, 128))
+    v.valid_s[...] = alive_rows * alive
+
+    for copy in arriving["bias"]:
+        copy.wait_recv()
+    for t in range(T):
+        for q in range(Q):
+            pieces = []
+            for b in range(B):
+                tile = v.bias_all[b // AX, b % AX, :, t * 128 : (t + 1) * 128]
+                turn = (b - q) % Q * J
+                pieces.append(pltpu.roll(tile, turn, 1) if turn else tile)
+            row = (t * Q + q) * H
+            v.bias_s[row : row + H, :] = joined(pieces, J)
+
+    def triangle(h):
+        for copy in sides[h]:
+            copy.wait_recv()
+        for z in range(R):
+            for t in range(0, T, 2):
+                rows = slice(t * 8, t * 8 + 16)
+                pieces = [v.side_all[h, b // AX, b % AX, z, rows, :].astype(f32) for b in range(B)]
+                for q, piece in enumerate(lane_exchange(pieces, J)):
+                    v.side_s[q, z * T * 8 + t * 8 : z * T * 8 + t * 8 + 16, :] = piece
+        for c in range(P4):
+            left, right = [
+                jnp.concatenate([v.side_s[q, pl.ds(side * P4 + c, R * T, stride=8), :] for q in range(Q)], axis=0)
+                for side in range(2)
+            ]
+            left = (left * v.depth_valid_s[...]).astype(bf16)
+            grid = dot(jnp.transpose(right).astype(bf16), left, ((1,), (0,))) * v.valid_s[...]
+            for b in range(B):
+                tiles = [grid[b * J + g * M : b * J + (g + 1) * M, :] for g in range(Q)]
+                for n, tile in enumerate(lane_exchange(tiles, J)):
+                    v.product_s[n, b // AX, b % AX, c * M : (c + 1) * M, :] = tile
+        v.product_own[h] = v.product_s[...].astype(bf16)
+        copies = share(v.product_own, v.product_all, v.product_send, v.product_recv, h)
+        v.product_all[h, p.r, p.b, p.x] = v.product_own[h, p.r, p.b, p.x]
+        return copies
+
+    products = triangle(0)
+
+    for copy in arriving["rows"]:
+        copy.wait_recv()
+    v.key_value_s[...] = (
+        dot(v.rows_all[...].reshape(R * S * A, F), v.row_in[:, F : 3 * F], ((1,), (0,)))
+        .astype(bf16)
+        .reshape(R, S * A, 2 * F)
+    )
+    presence = joined([v.row_present[n] for n in range(R)], A)
+    for s in range(S):
+        mine = slice(s * A, (s + 1) * A)
+        keys = v.key_value_s[:, mine, :F].reshape(R * A, F)
+        values = v.key_value_s[:, mine, F:].reshape(R * A, F)
+        scores = dot(by_head(query[mine], H).astype(bf16), keys, ((1,), (1,))) * scale
+        scores = scores + v.bias_s[...] + masked_fill_value * (presence[s : s + 1] - 1.0)
+        v.context_s[mine, :] = attend(scores, values, H)
+    loads["row_exit"].wait()
+    loads["col_in"].wait()
+    row_mix = (row_gate * v.context_s[...]).astype(bf16)
+    after_row = v.embedded_s[...] + dot(row_mix, v.row_exit[...], ((1,), (0,)))
+    normed_second = normalize(after_row).astype(bf16)
+    v.keys_own[...] = dot(normed_second, v.col_in[:, F : 3 * F], ((1,), (0,))).astype(bf16).reshape(S, A, 2 * F)
+
+    def pass_on(a):
+        origin = (p.b, p.aux_back(a))
+        src = v.keys_own if a == 0 else v.keys_all.at[origin]
+        for bo in range(1, BR):
+            copy = remote(src, v.keys_all.at[origin], v.over_send.at[a, bo], v.over_recv.at[a, bo], {"br": p.br(bo)})
+            sent.append(copy)
+            arriving["keys"].append(copy)
+
+    across = {}
+    for a in range(1, AX):
+        across[a] = remote(
+            v.keys_own, v.keys_all.at[p.b, p.x], v.across_send.at[a], v.across_recv.at[a], {"aux": p.aux(a)}
+        )
+        sent.append(across[a])
+    pass_on(0)
+    v.keys_all[p.b, p.x] = v.keys_own[...]
+    query = dot(normed_second, v.col_in[:, :F], ((1,), (0,))).astype(bf16).astype(f32)
+    col_gate = jax.nn.sigmoid(dot(normed_second, v.col_in[:, 3 * F :], ((1,), (0,))))
+
+    for h in range(1, rounds):
+        products += triangle(h)
+    for a in range(1, AX):
+        across[a].wait_recv()
+        pass_on(a)
+    for copy in arriving["keys"]:
+        copy.wait_recv()
+    presence = joined([v.col_present[b // AX, b % AX] for b in range(B)], S * N)
+    for g in range(A // N):
+        keys = v.keys_all[:, :, :, g * N : (g + 1) * N, :F].reshape(B * S * N, F)
+        values = v.keys_all[:, :, :, g * N : (g + 1) * N, F:].reshape(B * S * N, F)
+        rows = jnp.concatenate([query[s * A + g * N : s * A + (g + 1) * N] for s in range(S)], axis=0)
+        scores = dot(by_head(rows, H).astype(bf16), keys, ((1,), (1,))) * scale
+        scores = scores + masked_fill_value * (presence[g : g + 1] - 1.0)
+        scores = jnp.where(iota(scores.shape, 0) // H % N == iota(scores.shape, 1) % N, scores, -1e30)
+        context = attend(scores, values, H)
+        for s in range(S):
+            v.context_s[s * A + g * N : s * A + (g + 1) * N, :] = context[s * N : (s + 1) * N]
+    for name in ("col_exit", "feed_first", "feed_second", "tri_exit"):
+        loads[name].wait()
+    col_mix = (col_gate * v.context_s[...]).astype(bf16)
+    after_col = after_row + dot(col_mix, v.col_exit[...], ((1,), (0,)))
+    normed_third = normalize(after_col).astype(bf16)
+    hidden = jnp.maximum(dot(normed_third, v.feed_first[...], ((1,), (0,))), 0.0).astype(bf16)
+    v.alignment[...] = (after_col + dot(hidden, v.feed_second[...], ((1,), (0,)))).astype(bf16)
+
+    for copy in products:
+        copy.wait_recv()
+    normed = normalize(v.product_all[...].astype(f32).reshape(C, M, 128), axis=0)
+    v.final_s[...] = normed.reshape(C * M, 128)
+    for m in range(M):
+        turned = jnp.transpose(v.final_s[pl.ds(m, C, stride=M), :]).astype(bf16)
+        update = dot(turned, v.tri_exit[...], ((1,), (0,)))
+        for g in range(Q):
+            v.update_s[pl.ds(g * M + m, I, stride=J), :] = update[g * I : (g + 1) * I]
+    v.pair[...] = (v.couple[...].astype(f32) + v.gate_s[...] * v.update_s[...]).astype(bf16)
+    for copy in sent:
+        copy.wait_send()
+
+
+def hand_over(alignment, pair, alignment_out, pair_out, sem):
+    copies = [
+        pltpu.make_async_copy(alignment, alignment_out, sem.at[0]),
+        pltpu.make_async_copy(pair, pair_out, sem.at[1]),
+    ]
+    for copy in copies:
+        copy.start()
+    for copy in copies:
+        copy.wait()
+
+
+INPUTS = (
+    "couple", "tri_in", "homolog", "symbols", "entries", "table", "logit", "amino", "row_in", "row_exit", "col_in",
+    "col_exit", "feed_first", "feed_second", "tri_exit",
+)
+
+
+def far_first(count):
+    return sorted(range(count), key=lambda d: -min(d, count - d))
+
+
+def exchanged(sizes, inputs, dims):
+    R, BR, AX = sizes
+    B = BR * AX
+    S, A, F, H, I, J, C, P4, T, N, rounds = dims
+    M = J * J // 128
+    peers = R * B - 1
+    scratch = {name: pltpu.VMEM(inputs[name].shape, inputs[name].dtype) for name in INPUTS}
+    for name, shape, kind in (
+        ("side_own", (rounds, R, BR, AX, 8 * T, 128), bf16), ("side_all", (rounds, BR, AX, R, 8 * T, 128), bf16),
+        ("side_s", (B, R * T * 8, 128), f32),
+        ("product_s", (R, BR, AX, P4 * M, 128), f32), ("product_own", (rounds, R, BR, AX, P4 * M, 128), bf16),
+        ("product_all", (rounds, R, BR, AX, P4 * M, 128), bf16),
+        ("rows_own", (S * A, F), bf16), ("rows_all", (R, S * A, F), bf16),
+        ("present", (2, 8, 128), f32), ("row_present", (R, 8, 128), f32), ("col_present", (BR, AX, 8, 128), f32),
+        ("bias_own", (H, I * J), f32), ("bias_all", (BR, AX, H, I * J), f32), ("bias_s", (I * H, B * J), f32),
+        ("keys_own", (S, A, 2 * F), bf16), ("keys_all", (BR, AX, S, A, 2 * F), bf16),
+        ("key_value_s", (R, S * A, 2 * F), bf16), ("embedded_s", (S * A, F), f32), ("context_s", (S * A, F), f32),
+        ("pair_norm_s", (I * J, C), bf16), ("gate_s", (I * J, C), f32),
+        ("depth_valid_s", (128, 128), f32), ("valid_s", (128, 128), f32),
+        ("final_s", (C * M, 128), f32), ("update_s", (I * J, C), f32),
+    ):
+        scratch[name] = pltpu.VMEM(shape, kind)
+    for name, shape in (
+        ("side_send", (rounds, peers)), ("side_recv", (rounds, peers)),
+        ("product_send", (rounds, peers)), ("product_recv", (rounds, peers)),
+        ("row_send", (2, R)), ("row_recv", (2, R)), ("grp_send", (2, B)), ("grp_recv", (2, B)),
+        ("across_send", (AX,)), ("across_recv", (AX,)), ("over_send", (AX, BR)), ("over_recv", (AX, BR)),
+        ("load_sem", (len(INPUTS),)),
+    ):
+        scratch[name] = pltpu.SemaphoreType.DMA(shape)
+    names = [name + "_far" for name in INPUTS] + ["alignment", "pair", *scratch]
+    vmem = pl.BlockSpec(memory_space=pltpu.VMEM)
+    far = pl.BlockSpec(memory_space=pltpu.HBM)
+    shapes = [jax.ShapeDtypeStruct((S * A, F), bf16), jax.ShapeDtypeStruct((I * J, C), bf16)]
+    results = pl.pallas_call(
+        functools.partial(exchange_kernel, sizes, dims, names),
+        name="exchange",
+        out_shape=shapes,
+        in_specs=[far] * len(INPUTS),
+        out_specs=[vmem] * 2,
+        scratch_shapes=list(scratch.values()),
+        compiler_params=pltpu.CompilerParams(
+            collective_id=1, has_side_effects=True, vmem_limit_bytes=32 * 1024 * 1024
+        ),
+    )(*[pltpu.with_memory_space_constraint(inputs[name], pltpu.HBM) for name in INPUTS])
+    return pl.pallas_call(
+        hand_over,
+        name="hand_over",
+        out_shape=shapes,
+        in_specs=[vmem] * 2,
+        out_specs=[far] * 2,
+        scratch_shapes=[pltpu.SemaphoreType.DMA((2,))],
+        compiler_params=pltpu.CompilerParams(vmem_limit_bytes=4 * 1024 * 1024),
+    )(*results)
+
+
 def on_device(
     sizes,
     homolog_features,
@@ -399,6 +726,19 @@
     per = C // R
     T = I * J // 128
     N = 16
+    P4 = 4
+    if R == B == 128 // J and I == J and T % 2 == 0 and C % (P4 * R * B) == 0 and R * T * (128 // J) == 128:
+        inputs = {
+            "couple": couple_features.reshape(I * J, C), "tri_in": trimul_entry_matrix,
+            "homolog": homolog_features.reshape(S * A, F), "symbols": symbol_ids, "entries": entry_present,
+            "table": symbol_lookup_matrix, "logit": jnp.transpose(couple_logit_matrix),
+            "amino": amino_present.reshape(1, -1), "row_in": horizontal_entry_matrix,
+            "row_exit": horizontal_exit_matrix, "col_in": vertical_entry_matrix, "col_exit": vertical_exit_matrix,
+            "feed_first": feedforward_first_matrix, "feed_second": feedforward_second_matrix,
+            "tri_exit": trimul_exit_matrix,
+        }
+        alignment, pair = exchanged(sizes, inputs, (S, A, F, H, I, J, C, P4, T, N, C // (P4 * R * B)))
+        return (alignment.reshape(S, A, F), pair.reshape(I, J, C))
     assert I == J and R == B and 128 % J == 0 and 128 % A == 0 and 128 % (S * N) == 0 and A % N == 0
     M = J // (128 // J)
     near = (

time: 42.4 us -> 36.4 us (0.86)
  local copies, waits for them, and re-layouts: 4.54 us -> 0 us
  Pallas kernels: 37 us -> 35.6 us
    unnamed x5 -> x0, local copies, waits for them, and re-layouts: 4.54 us -> none
    pallas_call x1 -> x2, Pallas kernels: 37 us -> 35.6 us  [the longest x1 34.9 us: exchanged(): pl.pallas_call(functools.partial(exchange_kernel, sizes, dims, names), na...]
where the time goes in v1:
time: 36.4 us; the launch traced here: 36.3 us
  Pallas kernels  35.6 us (98%)
  between operations  0.64 us (2%)
    pallas_call x1, Pallas kernels, exchanged(): pl.pallas_call(functools.partial(exchange_kernel, sizes, dims, names), na...  34.9 us
    pallas_call x1, Pallas kernels, exchanged(): pl.pallas_call(hand_over, name='hand_over', out_shape=shapes, in_specs=[v...  0.74 us

profile of v1, /device:TPU:0, one launch (start us, length us, event | category | flops | bytes accessed | tf_op | source)
XLA Modules:
  0.0 36.3 jit_solution(1668844592997589783)
XLA Ops:
  0.6 34.9 %exchange.1 = (bf16[128,256]{1,0:T(8,128)(2,1)S(1)}, bf16[1024,128]{1,0:T(8,128)(2,1)S(1)}) custom-call(bf16[1024,128]{1,0:T(8,128)(2,1)} %bitcast.6, bf16[128,640]{1,0:T(8,128)(2,1)} %refs_1_.1, bf16[128,256]{1,0:T(8,128)(2,1)} %bitcast.7, s32[4,32]{1,0:T(4,128)} %refs_3_.1, s32[4,32]{1,0:T(4,128)} %refs_4_.1, bf16[23,256]{1,0:T(8,128)(2,1)} %refs_5_.1, ...), custom_call_target="tpu_custom_call" | custom-call | tf_op jit(solution)/shard_map/exchange/pallas_call | solution.py:681
  35.5 0.7 %hand_over.1 = (bf16[128,256]{1,0:T(8,128)(2,1)}, bf16[1024,128]{1,0:T(8,128)(2,1)}) custom-call(bf16[128,256]{1,0:T(8,128)(2,1)S(1)} %get-tuple-element.6.alignment, bf16[1024,128]{1,0:T(8,128)(2,1)S(1)} %get-tuple-element.7.pair), custom_call_target="tpu_custom_call" | custom-call | tf_op jit(solution)/shard_map/hand_over/pallas_call | solution.py:692

commit v2 on v1

--- a/solution.py
+++ b/solution.py
@@ -428,9 +428,11 @@
                 two = [value[n * 2 * P4 : (n + 1) * 2 * P4, u * 128 : (u + 1) * 128] for u in (t, t + 1)]
                 v.side_own[h, n // B, n // AX % BR, n % AX, t * 8 : t * 8 + 16, :] = jnp.concatenate(two, axis=0).astype(bf16)
 
-    def share(own, everyone, send, recv, h):
+    def share(own, everyone, send, recv, h, wanted=lambda a: True):
         copies = []
         for n, (d, bo, a) in enumerate(peers):
+            if not wanted(a):
+                continue
             to = (p.res(d), p.br(bo), p.aux(a))
             copy = remote(
                 own.at[(h, *to)], everyone.at[h, p.b, p.x, p.r] if everyone is v.side_all else everyone.at[h, p.r, p.b, p.x],
@@ -440,36 +442,62 @@
             sent.append(copy)
         return copies
 
+    def embed():
+        for name in ("homolog", "symbols", "entries", "table"):
+            loads[name].wait()
+        here = v.entries[...].astype(f32)
+        v.present[...] = jnp.zeros_like(v.present)
+        v.present[0, :S, :] = jnp.concatenate([here] * (128 // A), axis=1)
+        for g in range(A // N):
+            pieces = [here[s : s + 1, g * N : (g + 1) * N] for s in range(S)]
+            v.present[1, g : g + 1, :] = jnp.concatenate(pieces * (128 // (S * N)), axis=1)
+        tokens = v.table.shape[0]
+        for s in range(S):
+            chosen = (iota((tokens, A), 0) == v.symbols[s : s + 1, :]).astype(f32)
+            v.context_s[s * A : (s + 1) * A, :] = dot(jnp.transpose(chosen).astype(bf16), v.table[...], ((1,), (0,)))
+        embedded = v.homolog[...].astype(f32) + v.context_s[...]
+        v.embedded_s[...] = embedded
+        v.rows_own[...] = normalize(embedded).astype(bf16)
+
+    half = R // 2
+    upper = p.r // half
+    base = upper * half
+    gateway = p.r == half - 1 + upper
+    foreign = [(1 - upper) * half + k for k in range(half)]
+    mates = [base + lax.rem(p.r - base + e, half) for e in range(1, half)]
+
+    def row_copy(origin, to, send, own):
+        pairs = ((v.rows_own, v.rows_all), (v.present.at[0], v.row_present))
+        return [
+            pltpu.make_async_remote_copy(
+                src_ref=src if own else dst.at[origin], dst_ref=dst.at[origin],
+                send_sem=send.at[n], recv_sem=v.row_recv.at[n, origin], device_id={"res": to}, device_id_type=MESH,
+            )
+            for n, (src, dst) in enumerate(pairs)
+        ]
+
+    forwards = [
+        row_copy(origin, to, v.forward_send.at[k, e], False)
+        for k, origin in enumerate(foreign)
+        for e, to in enumerate(mates)
+    ]
+
+    def received(origins):
+        for origin in origins:
+            for copy in row_copy(origin, p.r, v.row_send.at[0], False):
+                copy.wait_recv()
+
     loads["couple"].wait()
     loads["tri_in"].wait()
     pair_norm = normalize(v.couple[...]).astype(bf16)
     v.pair_norm_s[...] = pair_norm
+    embed()
     operands(0, pair_norm)
     pl.semaphore_wait(barrier, D - 1)
-    sides = {0: share(v.side_own, v.side_all, v.side_send, v.side_recv, 0)}
-
-    for name in ("homolog", "symbols", "entries", "table"):
-        loads[name].wait()
-    here = v.entries[...].astype(f32)
-    v.present[...] = jnp.zeros_like(v.present)
-    v.present[0, :S, :] = jnp.concatenate([here] * (128 // A), axis=1)
-    for g in range(A // N):
-        pieces = [here[s : s + 1, g * N : (g + 1) * N] for s in range(S)]
-        v.present[1, g : g + 1, :] = jnp.concatenate(pieces * (128 // (S * N)), axis=1)
-    tokens = v.table.shape[0]
-    for s in range(S):
-        chosen = (iota((tokens, A), 0) == v.symbols[s : s + 1, :]).astype(f32)
-        v.context_s[s * A : (s + 1) * A, :] = dot(jnp.transpose(chosen).astype(bf16), v.table[...], ((1,), (0,)))
-    embedded = v.homolog[...].astype(f32) + v.context_s[...]
-    v.embedded_s[...] = embedded
-    normed_first = normalize(embedded).astype(bf16)
-    v.rows_own[...] = normed_first
-    for d in far_first(R):
-        if d:
-            for n, (src, dst) in enumerate(((v.rows_own, v.rows_all), (v.present.at[0], v.row_present))):
-                copy = remote(src, dst.at[p.r], v.row_send.at[n, d], v.row_recv.at[n, d], {"res": p.res(d)})
-                sent.append(copy)
-                arriving["rows"].append(copy)
+    for n, to in enumerate([half - upper, *mates]):
+        for copy in row_copy(p.r, to, v.row_send.at[n], True):
+            copy.start()
+            sent.append(copy)
     loads["logit"].wait()
     v.bias_own[...] = dot(v.logit[...], pair_norm, ((1,), (1,)))
     for n, (bo, a) in enumerate(p.group()):
@@ -478,9 +506,9 @@
             copy = remote(src, dst.at[p.b, p.x], v.grp_send.at[m, n], v.grp_recv.at[m, n], to)
             sent.append(copy)
             arriving["bias"].append(copy)
+    sides = {0: share(v.side_own, v.side_all, v.side_send, v.side_recv, 0)}
     for h in range(1, rounds):
         operands(h, v.pair_norm_s[...])
-        sides[h] = share(v.side_own, v.side_all, v.side_send, v.side_recv, h)
 
     v.rows_all[p.r] = v.rows_own[...]
     v.row_present[p.r] = v.present[0]
@@ -490,6 +518,7 @@
         v.side_all[h, p.b, p.x, p.r] = v.side_own[h, p.r, p.b, p.x]
 
     loads["row_in"].wait()
+    normed_first = v.rows_own[...]
     query = dot(normed_first, v.row_in[:, :F], ((1,), (0,))).astype(bf16).astype(f32)
     row_gate = jax.nn.sigmoid(dot(normed_first, v.row_in[:, 3 * F :], ((1,), (0,))))
     v.gate_s[...] = jax.nn.sigmoid(dot(v.pair_norm_s[...], v.tri_in[:, 4 * C :], ((1,), (0,))))
@@ -503,6 +532,15 @@
     v.depth_valid_s[...] = jnp.broadcast_to(alive_depth, (128, 128))
     v.valid_s[...] = alive_rows * alive
 
+    @pl.when(gateway)
+    def _():
+        received(foreign)
+        for copies in forwards:
+            for copy in copies:
+                copy.start()
+
+    for h in range(1, rounds):
+        sides[h] = share(v.side_own, v.side_all, v.side_send, v.side_recv, h)
     for copy in arriving["bias"]:
         copy.wait_recv()
     for t in range(T):
@@ -540,10 +578,11 @@
         v.product_all[h, p.r, p.b, p.x] = v.product_own[h, p.r, p.b, p.x]
         return copies
 
-    products = triangle(0)
-
-    for copy in arriving["rows"]:
-        copy.wait_recv()
+    @pl.when(jnp.logical_not(gateway))
+    def _():
+        received(foreign)
+
+    received(mates)
     v.key_value_s[...] = (
         dot(v.rows_all[...].reshape(R * S * A, F), v.row_in[:, F : 3 * F], ((1,), (0,)))
         .astype(bf16)
@@ -583,11 +622,12 @@
     query = dot(normed_second, v.col_in[:, :F], ((1,), (0,))).astype(bf16).astype(f32)
     col_gate = jax.nn.sigmoid(dot(normed_second, v.col_in[:, 3 * F :], ((1,), (0,))))
 
-    for h in range(1, rounds):
-        products += triangle(h)
+    products = triangle(0)
     for a in range(1, AX):
         across[a].wait_recv()
         pass_on(a)
+    for h in range(1, rounds):
+        products += triangle(h)
     for copy in arriving["keys"]:
         copy.wait_recv()
     presence = joined([v.col_present[b // AX, b % AX] for b in range(B)], S * N)
@@ -609,6 +649,16 @@
     hidden = jnp.maximum(dot(normed_third, v.feed_first[...], ((1,), (0,))), 0.0).astype(bf16)
     v.alignment[...] = (after_col + dot(hidden, v.feed_second[...], ((1,), (0,)))).astype(bf16)
 
+    waiting = len(sent) - (rounds - 1) * (D - 1)
+    for copy in sent[:waiting]:
+        copy.wait_send()
+
+    @pl.when(gateway)
+    def _():
+        for copies in forwards:
+            for copy in copies:
+                copy.wait_send()
+
     for copy in products:
         copy.wait_recv()
     normed = normalize(v.product_all[...].astype(f32).reshape(C, M, 128), axis=0)
@@ -619,7 +669,7 @@
         for g in range(Q):
             v.update_s[pl.ds(g * M + m, I, stride=J), :] = update[g * I : (g + 1) * I]
     v.pair[...] = (v.couple[...].astype(f32) + v.gate_s[...] * v.update_s[...]).astype(bf16)
-    for copy in sent:
+    for copy in sent[waiting:]:
         copy.wait_send()
 
 
@@ -669,7 +719,7 @@
     for name, shape in (
         ("side_send", (rounds, peers)), ("side_recv", (rounds, peers)),
         ("product_send", (rounds, peers)), ("product_recv", (rounds, peers)),
-        ("row_send", (2, R)), ("row_recv", (2, R)), ("grp_send", (2, B)), ("grp_recv", (2, B)),
+        ("row_send", (R // 2, 2)), ("row_recv", (2, R)), ("forward_send", (R // 2, R // 2, 2)), ("grp_send", (2, B)), ("grp_recv", (2, B)),
         ("across_send", (AX,)), ("across_recv", (AX,)), ("over_send", (AX, BR)), ("over_recv", (AX, BR)),
         ("load_sem", (len(INPUTS),)),
     ):

time: 36.4 us -> 35 us (0.962)
  Pallas kernels: 35.6 us -> 34.2 us
    pallas_call x1, Pallas kernels: 34.9 us -> 33.5 us  [exchanged(): pl.pallas_call(functools.partial(exchange_kernel, sizes, dims, names), na...]
where the time goes in v2:
time: 35 us; the launch traced here: 34.9 us
  Pallas kernels  34.2 us (98%)
  between operations  0.64 us (2%)
    pallas_call x1, Pallas kernels, exchanged(): pl.pallas_call(functools.partial(exchange_kernel, sizes, dims, names), na...  33.5 us
    pallas_call x1, Pallas kernels, exchanged(): pl.pallas_call(hand_over, name='hand_over', out_shape=shapes, in_specs=[v...  0.74 us

profile of v2, /device:TPU:0, one launch (start us, length us, event | category | flops | bytes accessed | tf_op | source)
XLA Modules:
  0.0 34.9 jit_solution(14456744219936435621)
XLA Ops:
  0.6 33.5 %exchange.1 = (bf16[128,256]{1,0:T(8,128)(2,1)S(1)}, bf16[1024,128]{1,0:T(8,128)(2,1)S(1)}) custom-call(bf16[1024,128]{1,0:T(8,128)(2,1)} %bitcast.6, bf16[128,640]{1,0:T(8,128)(2,1)} %refs_1_.1, bf16[128,256]{1,0:T(8,128)(2,1)} %bitcast.7, s32[4,32]{1,0:T(4,128)} %refs_3_.1, s32[4,32]{1,0:T(4,128)} %refs_4_.1, bf16[23,256]{1,0:T(8,128)(2,1)} %refs_5_.1, ...), custom_call_target="tpu_custom_call" | custom-call | tf_op jit(solution)/shard_map/exchange/pallas_call | solution.py:731
  34.1 0.7 %hand_over.1 = (bf16[128,256]{1,0:T(8,128)(2,1)}, bf16[1024,128]{1,0:T(8,128)(2,1)}) custom-call(bf16[128,256]{1,0:T(8,128)(2,1)S(1)} %get-tuple-element.6.alignment, bf16[1024,128]{1,0:T(8,128)(2,1)S(1)} %get-tuple-element.7.pair), custom_call_target="tpu_custom_call" | custom-call | tf_op jit(solution)/shard_map/hand_over/pallas_call | solution.py:742
